TPU v7x, 32 devices: a whole 2x2x4 slice. The times are simulated.
32 devices in a mesh: energy: 8 (over z, core), momentum: 4 (over y, x).
Axes of the slice: x: 2, y: 2, z: 4, core: 2. Of those that a mesh axis runs over, the one named last changes fastest.
Arguments:
- hopping: float32 [4, 2, 2, 384, 384], P('momentum'), may hold values from -0.07 to 0.07, as said below
- coupling: float32 [4, 2, 384, 384], P('momentum'), may hold values from -0.15 to 0.15
- onsite: float32 [2, 384], replicated, may hold values from -4 to -2.5
- sigma_in: float32 [8, 4, 2, 147456], P('energy', 'momentum'), may hold values from -0.12 to 0.12
- neighbor_shift: int32 [96, 48], replicated, may hold values from 1 to 95
- mode_shift: int32 [6], replicated, may hold values from 1 to 3
- phonon_kernel: float32 [6, 2, 4, 4], replicated, may hold values from -240 to 240
Outputs:
- sigma_new: float32 [8, 4, 2, 147456], P('energy', 'momentum')
Inputs may be any that keep to these rules, and one draw needn't show every extreme that they name: hopping[k, c, 0] is symmetric with a zero diagonal and hopping[k, c, 1] is antisymmetric, so every cell block is Hermitian.
All inputs are finite; a program needn't handle non-finite values.
Results may differ from a plain program's by a relative error of at most 0.0003.
Values sent between devices are 32-bit elements; how exact they have to be, the bound alone decides.
A program may use at most 256 MiB of HBM per device.

v0:
```python
import functools

import jax
import jax.numpy as jnp
from jax import lax
from jax.experimental import pallas as pl
from jax.experimental.pallas import tpu as pltpu
from jax.sharding import PartitionSpec as P

BROADENING = 0.5
LANES = 128
F32 = jnp.float32
BF16 = jnp.bfloat16


def dot(a, b):
    return jnp.dot(a, b, preferred_element_type=F32)


def split(x):
    high = x.astype(BF16)
    return high, (x - high.astype(F32)).astype(BF16)


def point_kernel(
    dims, z_ref, pairs_ref, shift_ref, hop_ref, coup_ref, onsite_ref, out_ref,
    rows_ref, sig_ref, acc_ref, coupling, adjoint, system, guess, prod, first, second, ag,
    left_h, left_l, right_h, right_l,
):
    atoms, neigh, per_atom = dims
    orb = atoms * per_atom
    entries = 2 * per_atom * per_atom
    groups = LANES // entries
    chunks = neigh // groups
    f32_lanes = lax.broadcasted_iota(jnp.int32, (atoms, LANES), 1)

    for cell in range(2):
        for chunk in range(chunks):
            part = pairs_ref[pl.ds(2 * chunk + cell, atoms, stride=2 * chunks), :]
            rows_ref[chunk * LANES:(chunk + 1) * LANES, 0:atoms] = part.T
        for entry in range(entries):
            part = rows_ref[pl.ds(entry, neigh, stride=entries), :]
            sig_ref[cell * entries + entry, :, 0:neigh] = part.T[0:atoms]

    index = lax.broadcasted_iota(jnp.int32, (atoms, neigh), 0) + shift_ref[...].T
    index = jnp.where(index >= atoms, index - atoms, index)

    def following(previous):
        current = jnp.full((atoms, LANES), LANES, jnp.int32)
        for n in reversed(range(neigh)):
            column = jnp.broadcast_to(index[:, n:n + 1], (atoms, LANES))
            current = jnp.where((column == f32_lanes) & (n > previous), n, current)
        return current

    def gathered(block, current):
        safe = jnp.where(current < LANES, current, 0)
        value = jnp.take_along_axis(sig_ref[block], safe, axis=1)
        return jnp.where(current < LANES, value, 0.0)

    def smallest(current):
        return jnp.min(current)

    current = following(jnp.full((atoms, LANES), -1, jnp.int32))

    unroll = 8

    def store_first(group, carry):
        for u in range(unroll):
            block = group * unroll + u
            acc_ref[block] = gathered(block, current)
        return carry

    lax.fori_loop(0, 2 * entries // unroll, store_first, 0)

    def more(state):
        return state[1] < LANES

    def step(state):
        now = state[0]

        def add(group, carry):
            for u in range(unroll):
                block = group * unroll + u
                acc_ref[block] = acc_ref[block] + gathered(block, now)
            return carry

        lax.fori_loop(0, 2 * entries // unroll, add, 0)
        later = following(now)
        return later, smallest(later)

    current = following(current)
    lax.while_loop(more, step, (current, smallest(current)))

    row = lax.broadcasted_iota(jnp.int32, (orb, orb), 0)
    col = lax.broadcasted_iota(jnp.int32, (orb, orb), 1)
    eye = row == col

    def source(position):
        turn = sum((position >= atoms * k).astype(jnp.int32) for k in range(1, per_atom))
        return per_atom * (position - atoms * turn) + turn

    perm = (col == source(row)).astype(F32).astype(BF16)
    perm_t = (row == source(col)).astype(F32).astype(BF16)

    def permuted(matrix):
        high, low = split(matrix)
        moved = dot(perm, jnp.concatenate([high, low], axis=1)).astype(BF16)
        return dot(moved[:, 0:orb], perm_t) + dot(moved[:, orb:], perm_t)

    def put_left(ref):
        high, low = split(ref[...])
        left_h[...] = high
        left_l[...] = low

    def put_right(ref):
        high, low = split(ref[...])
        for part, dst in ((high, right_h), (low, right_l)):
            dst[0:orb, :] = part
            dst[orb:2 * orb, 0:orb] = -part[:, orb:]
            dst[orb:2 * orb, orb:] = part[:, 0:orb]

    width = 256 if (2 * orb) % 256 == 0 else LANES

    def product(emit):
        def tile(t, carry):
            window = pl.ds(pl.multiple_of(t * width, width), width)
            high = right_h[:, window]
            total = dot(left_h[...], right_l[:, window]) + dot(left_l[...], high)
            emit(window, total + dot(left_h[...], high))
            return carry

        lax.fori_loop(0, 2 * orb // width, tile, 0)

    def into(dst):
        def emit(window, value):
            dst[:, window] = value
        return emit

    def invert(dst):
        real, imag = system[:, 0:orb], system[:, orb:]
        own_real, own_imag = jnp.where(eye, real, 0.0), jnp.where(eye, imag, 0.0)
        pairs = []
        for axis in (0, 1):
            dr = jnp.sum(own_real, axis=axis, keepdims=True)
            di = jnp.sum(own_imag, axis=axis, keepdims=True)
            size = dr * dr + di * di
            pairs.append((dr / size, -di / size))
        (rr, ri), (cr, ci) = pairs
        col_real, col_imag = real * rr - imag * ri, real * ri + imag * rr
        guess[:, 0:orb] = jnp.where(eye, 2.0 * rr, 0.0) - (cr * col_real - ci * col_imag)
        guess[:, orb:] = jnp.where(eye, 2.0 * ri, 0.0) - (cr * col_imag + ci * col_real)
        put_left(system)
        put_right(guess)
        product(into(prod))
        put_left(guess)
        put_right(prod)

        def emit(window, value):
            dst[:, window] = 2.0 * guess[:, window] - value

        product(emit)

    def build_system(cell):
        onsite = jnp.where(eye, onsite_ref[cell:cell + 1, :], 0.0)
        system[:, 0:orb] = jnp.where(eye, z_ref[0], 0.0) - permuted(hop_ref[0, cell, 0] + onsite)
        system[:, orb:] = jnp.where(eye, BROADENING, 0.0) - permuted(hop_ref[0, cell, 1])
        for part in range(2):
            for i in range(per_atom):
                blocks = []
                for j in range(per_atom):
                    entry = ((cell * 2 + part) * per_atom + i) * per_atom + j
                    blocks.append(acc_ref[entry][:, 0:atoms])
                band = (slice(i * atoms, (i + 1) * atoms), slice(part * orb, (part + 1) * orb))
                system[band] = system[band] - jnp.concatenate(blocks, axis=1)

    coup_real, coup_imag = permuted(coup_ref[0, 0]), permuted(coup_ref[0, 1])
    coupling[:, 0:orb] = coup_real
    coupling[:, orb:] = coup_imag
    adjoint[:, 0:orb] = coup_real.T
    adjoint[:, orb:] = -coup_imag.T

    build_system(0)
    invert(first)
    put_left(adjoint)
    put_right(first)
    product(into(ag))
    build_system(1)
    put_left(ag)
    put_right(coupling)

    def fold(window, value):
        system[:, window] = system[:, window] - value

    product(fold)
    put_left(first)
    product(into(adjoint))
    invert(second)
    put_left(adjoint)
    put_right(second)
    product(into(prod))
    put_left(prod)
    put_right(ag)

    def full(window, value):
        first[:, window] = first[:, window] + value

    product(full)

    pad = jnp.zeros((atoms, LANES - neigh), jnp.int32)
    pick = jnp.concatenate([index, pad], axis=1)
    for cell, green in ((0, first), (1, second)):
        for part in range(2):
            for i in range(per_atom):
                for j in range(per_atom):
                    start = part * orb + j * atoms
                    lane = min(start, 2 * orb - LANES)
                    block = green[i * atoms:(i + 1) * atoms, lane:lane + LANES]
                    value = jnp.take_along_axis(block, pick + (start - lane), axis=1)
                    entry = (part * per_atom + i) * per_atom + j
                    value = jnp.concatenate([value, jnp.zeros((LANES - atoms, LANES), F32)], axis=0)
                    rows_ref[pl.ds(entry, neigh, stride=entries), :] = value.T[0:neigh]
        for chunk in range(chunks):
            part = rows_ref[chunk * LANES:(chunk + 1) * LANES, :].T
            out_ref[pl.ds(2 * chunk + cell, atoms, stride=2 * chunks), :] = part[0:atoms]


def green_pairs_of(energy_real, pairs, neighbor_shift, hopping, coupling, onsite, per_atom):
    neigh, atoms = neighbor_shift.shape
    orb = atoms * per_atom
    entries = 2 * per_atom * per_atom
    vmem = pl.BlockSpec(memory_space=pltpu.VMEM)
    complex_block = pltpu.VMEM((orb, 2 * orb), F32)
    return pl.pallas_call(
        functools.partial(point_kernel, (atoms, neigh, per_atom)),
        out_shape=jax.ShapeDtypeStruct(pairs.shape, F32),
        in_specs=[pl.BlockSpec(memory_space=pltpu.SMEM)] + [vmem] * 5,
        out_specs=vmem,
        scratch_shapes=[
            pltpu.VMEM((neigh * entries, LANES), F32),
            pltpu.VMEM((2 * entries, atoms, LANES), F32),
            pltpu.VMEM((2 * entries, atoms, LANES), F32),
        ]
        + [complex_block] * 8
        + [pltpu.VMEM((orb, 2 * orb), BF16)] * 2
        + [pltpu.VMEM((2 * orb, 2 * orb), BF16)] * 2,
        compiler_params=pltpu.CompilerParams(vmem_limit_bytes=60 * 1024 * 1024),
        name="point_green",
    )(energy_real, pairs, neighbor_shift, hopping, coupling, onsite)


def mix_kernel(weight_ref, x_ref, o_ref):
    points = x_ref.shape[0]

    def target(p, carry):
        total = weight_ref[p, 0] * x_ref[0]
        for q in range(1, points):
            total = total + weight_ref[p, q] * x_ref[q]
        o_ref[p] = total
        return carry

    lax.fori_loop(0, points, target, 0)


def mix(weights, received):
    return pl.pallas_call(
        mix_kernel,
        out_shape=jax.ShapeDtypeStruct(received.shape, F32),
        in_specs=[pl.BlockSpec(memory_space=pltpu.SMEM), pl.BlockSpec(memory_space=pltpu.VMEM)],
        out_specs=pl.BlockSpec(memory_space=pltpu.VMEM),
        name="mix_points",
    )(weights, received)


def build_kernel(mode_shift, phonon_kernel, energies, momenta):
    modes = mode_shift.shape[0]
    target = lax.broadcasted_iota(jnp.int32, (modes, energies, energies), 1)
    source = lax.broadcasted_iota(jnp.int32, (modes, energies, energies), 2)
    shifted = mode_shift[:, None, None]
    lower = (source == target - shifted).astype(F32)
    upper = (source == target + shifted).astype(F32)
    high = lax.Precision.HIGHEST
    combined = jnp.einsum("jab,jkq->akbq", lower, phonon_kernel[:, 0], precision=high)
    combined = combined + jnp.einsum("jab,jkq->akbq", upper, phonon_kernel[:, 1], precision=high)
    return combined.reshape(energies * momenta, energies * momenta)


def body(hopping, coupling, onsite, sigma_in, neighbor_shift, mode_shift, phonon_kernel):
    energies = sigma_in.shape[0] * lax.axis_size("energy")
    momenta = sigma_in.shape[1] * lax.axis_size("momentum")
    points = energies * momenta
    pair_cols = sigma_in.shape[3]
    atoms = neighbor_shift.shape[0]
    per_atom = onsite.shape[1] // atoms
    energy_real = 2.0 * (lax.axis_index("energy").astype(F32) + 0.5) / energies
    pairs = sigma_in.reshape(2, pair_cols // LANES, LANES).transpose(1, 0, 2)
    pairs = pairs.reshape(2 * pair_cols // LANES, LANES)
    green = green_pairs_of(
        energy_real.reshape(1), pairs, neighbor_shift.T, hopping, coupling, onsite, per_atom
    )
    weights = build_kernel(mode_shift, phonon_kernel, energies, momenta)
    blocks = green.reshape(points, 2 * pair_cols // LANES // points, LANES)
    names = ("energy", "momentum")
    received = lax.all_to_all(blocks, names, split_axis=0, concat_axis=0, tiled=True)
    mixed = mix(weights, received)
    returned = lax.all_to_all(mixed, names, split_axis=0, concat_axis=0, tiled=True)
    returned = returned.reshape(pair_cols // LANES, 2, LANES).transpose(1, 0, 2)
    return returned.reshape(1, 1, 2, pair_cols)


def solution(mesh):
    return jax.shard_map(
        body,
        mesh=mesh,
        in_specs=(
            P("momentum", None, None, None, None),
            P("momentum", None, None, None),
            P(),
            P("energy", "momentum", None, None),
            P(),
            P(),
            P(),
        ),
        out_specs=P("energy", "momentum", None, None),
        check_vma=False,
    )
```

profile of v0, /device:TPU:0, one launch (start us, length us, event | category | flops | bytes accessed | tf_op | source)
XLA Modules:
  0.0 134.1 jit_solution(1943968444714521528)
XLA Ops:
  0.0 55.8 %point_green.1 = f32[2304,128]{1,0:T(8,128)} custom-call(f32[1]{0:T(128)} %bitcast.9.z_ref, f32[2304,128]{1,0:T(8,128)} %bitcast.37, s32[48,96]{1,0:T(8,128)} %bitcast.38, f32[1,2,2,384,384]{4,3,2,1,0:T(8,128)} %hop_ref.1, f32[1,2,384,384]{3,2,1,0:T(8,128)} %coup_ref.1, f32[2,384]{1,0:T(2,128)} %onsite_ref.1), custom_call_target="tpu_custom_call" | custom-call | tf_op jit(solution)/shard_map/point_green/pallas_call | solution.py:233
  55.8 0.0 copy-start.1
  55.8 0.0 copy-start.2
  55.8 7.3 %all-to-all-start = ((f32[32,72,128]{2,1,0:T(8,128)}), f32[32,72,128]{2,1,0:T(8,128)S(1)}, u32[]{:S(2)}, u32[]{:S(2)}) async-start(f32[32,72,128]{2,1,0:T(8,128)} %bitcast.36), calls=%async_computation | async-start | bytes 2359296 | tf_op jit(solution)/shard_map/all_to_all | solution.py:303
  63.1 0.0 copy-done.1
  63.1 0.0 copy-done.2
  63.1 0.3 fusion.2
  63.4 0.3 fusion
  63.7 0.3 copy.11
  63.9 0.7 reshape.22.weight_ref
  64.6 27.6 %all-to-all-done.x_ref = f32[32,72,128]{2,1,0:T(8,128)S(1)} async-done(((f32[32,72,128]{2,1,0:T(8,128)}), f32[32,72,128]{2,1,0:T(8,128)S(1)}, u32[]{:S(2)}, u32[]{:S(2)}) %all-to-all-start) | async-done | bytes 1179680 | tf_op jit(solution)/shard_map/all_to_all | solution.py:303
  92.2 0.0 copy-start
  92.2 1.0 copy-done
  93.2 5.5 %mix_points.1 = f32[32,72,128]{2,1,0:T(8,128)} custom-call(f32[32,32]{1,0:T(8,128)} %reshape.22.weight_ref, f32[32,72,128]{2,1,0:T(8,128)} %copy-done), custom_call_target="tpu_custom_call" | custom-call | tf_op jit(solution)/shard_map/mix_points/pallas_call | solution.py:265
  98.8 34.3 %all_to_all.10 = f32[32,72,128]{2,1,0:T(8,128)S(1)} all-to-all(f32[32,72,128]{2,1,0:T(8,128)} %mix_points.1), channel_id=1, replica_groups=mesh['energy'=8,'momentum'=4] {'energy','momentum'}, dimensions={0} | all-to-all | bytes 2359296 | tf_op jit(solution)/shard_map/all_to_all | solution.py:305
  133.1 1.0 copy.17
Async XLA Ops:
  55.8 7.3 %copy-start.1 = (f32[6,2,4,4]{0,3,2,1:T(4,128)S(1)}, f32[6,2,4,4]{0,3,2,1:T(4,128)}, u32[]{:S(2)}) copy-start(f32[6,2,4,4]{0,3,2,1:T(4,128)} %param.13) | copy-start | bytes 2308
  55.8 7.3 %copy-start.2 = (s32[6]{0:T(128)S(1)}, s32[6]{0:T(128)}, u32[]{:S(2)}) copy-start(s32[6]{0:T(128)} %param.12) | copy-start | bytes 76
  55.8 36.4 %all-to-all-start = ((f32[32,72,128]{2,1,0:T(8,128)}), f32[32,72,128]{2,1,0:T(8,128)S(1)}, u32[]{:S(2)}, u32[]{:S(2)}) async-start(f32[32,72,128]{2,1,0:T(8,128)} %bitcast.36), calls=%async_computation | async-start | bytes 2359296 | tf_op jit(solution)/shard_map/all_to_all | solution.py:303
  92.2 1.0 copy-start
where the time goes:
time: 134 us
  Pallas kernels  61.3 us (46%)
  blocking collectives  34.3 us (26%)
  waiting for transfers between devices  27.6 us (21%)
  starting transfers between devices  7.32 us (5%)
  local copies, waits for them, and re-layouts  2.99 us (2%)
    pallas_call x1, Pallas kernels, green_pairs_of(): pl.pallas_call(functools.partial(point_kernel, (atoms, neigh, per_atom)),...  55.8 us
    all_to_all x1, blocking collectives, body(): lax.all_to_all(mixed, names, split_axis=0, concat_axis=0, tiled=True)  34.3 us
    all_to_all x1, waiting for transfers between devices, body(): lax.all_to_all(blocks, names, split_axis=0, concat_axis=0, tiled=True)  27.6 us
    all_to_all x1, starting transfers between devices, body(): lax.all_to_all(blocks, names, split_axis=0, concat_axis=0, tiled=True)  7.32 us
    pallas_call x1, Pallas kernels, mix(): pl.pallas_call(mix_kernel, out_shape=jax.ShapeDtypeStruct(received.shape,...  5.55 us
  transfers between devices with their start and end apart: 1, of which 1 were waited for; matrix products, arithmetic and copies ran while one was open for 1% of the time, Pallas kernels for 0%

commit v1 on v0

--- a/solution.py
+++ b/solution.py
@@ -122,14 +122,11 @@
     width = 256 if (2 * orb) % 256 == 0 else LANES
 
     def product(emit):
-        def tile(t, carry):
-            window = pl.ds(pl.multiple_of(t * width, width), width)
+        for t in range(2 * orb // width):
+            window = slice(t * width, (t + 1) * width)
             high = right_h[:, window]
             total = dot(left_h[...], right_l[:, window]) + dot(left_l[...], high)
             emit(window, total + dot(left_h[...], high))
-            return carry
-
-        lax.fori_loop(0, 2 * orb // width, tile, 0)
 
     def into(dst):
         def emit(window, value):

time: 134 us -> 124 us (0.925)
  Pallas kernels: 61.3 us -> 51 us
    pallas_call x1, Pallas kernels: 55.8 us -> 45.4 us  [green_pairs_of(): pl.pallas_call(functools.partial(point_kernel, (atoms, neigh, per_atom)),...]
where the time goes in v1:
time: 124 us
  Pallas kernels  51 us (41%)
  blocking collectives  34.3 us (28%)
  waiting for transfers between devices  27.6 us (22%)
  starting transfers between devices  7.32 us (6%)
  local copies, waits for them, and re-layouts  2.99 us (2%)
    pallas_call x1, Pallas kernels, green_pairs_of(): pl.pallas_call(functools.partial(point_kernel, (atoms, neigh, per_atom)),...  45.4 us
    all_to_all x1, blocking collectives, body(): lax.all_to_all(mixed, names, split_axis=0, concat_axis=0, tiled=True)  34.3 us
    all_to_all x1, waiting for transfers between devices, body(): lax.all_to_all(blocks, names, split_axis=0, concat_axis=0, tiled=True)  27.6 us
    all_to_all x1, starting transfers between devices, body(): lax.all_to_all(blocks, names, split_axis=0, concat_axis=0, tiled=True)  7.32 us
    pallas_call x1, Pallas kernels, mix(): pl.pallas_call(mix_kernel, out_shape=jax.ShapeDtypeStruct(received.shape,...  5.55 us
  transfers between devices with their start and end apart: 1, of which 1 were waited for; matrix products, arithmetic and copies ran while one was open for 1% of the time, Pallas kernels for 0%

profile of v1, /device:TPU:0, one launch (start us, length us, event | category | flops | bytes accessed | tf_op | source)
XLA Modules:
  0.0 123.7 jit_solution(8086299775699764615)
XLA Ops:
  0.0 45.4 %point_green.1 = f32[2304,128]{1,0:T(8,128)} custom-call(f32[1]{0:T(128)} %bitcast.9.z_ref, f32[2304,128]{1,0:T(8,128)} %bitcast.37, s32[48,96]{1,0:T(8,128)} %bitcast.38, f32[1,2,2,384,384]{4,3,2,1,0:T(8,128)} %hop_ref.1, f32[1,2,384,384]{3,2,1,0:T(8,128)} %coup_ref.1, f32[2,384]{1,0:T(2,128)} %onsite_ref.1), custom_call_target="tpu_custom_call" | custom-call | tf_op jit(solution)/shard_map/point_green/pallas_call | solution.py:230
  45.4 0.0 copy-start.1
  45.4 0.0 copy-start.2
  45.4 7.3 %all-to-all-start = ((f32[32,72,128]{2,1,0:T(8,128)}), f32[32,72,128]{2,1,0:T(8,128)S(1)}, u32[]{:S(2)}, u32[]{:S(2)}) async-start(f32[32,72,128]{2,1,0:T(8,128)} %bitcast.36), calls=%async_computation | async-start | bytes 2359296 | tf_op jit(solution)/shard_map/all_to_all | solution.py:300
  52.8 0.0 copy-done.1
  52.8 0.0 copy-done.2
  52.8 0.3 fusion.2
  53.0 0.3 fusion
  53.3 0.3 copy.11
  53.6 0.7 reshape.22.weight_ref
  54.3 27.6 %all-to-all-done.x_ref = f32[32,72,128]{2,1,0:T(8,128)S(1)} async-done(((f32[32,72,128]{2,1,0:T(8,128)}), f32[32,72,128]{2,1,0:T(8,128)S(1)}, u32[]{:S(2)}, u32[]{:S(2)}) %all-to-all-start) | async-done | bytes 1179680 | tf_op jit(solution)/shard_map/all_to_all | solution.py:300
  81.8 0.0 copy-start
  81.8 1.0 copy-done
  82.9 5.5 %mix_points.1 = f32[32,72,128]{2,1,0:T(8,128)} custom-call(f32[32,32]{1,0:T(8,128)} %reshape.22.weight_ref, f32[32,72,128]{2,1,0:T(8,128)} %copy-done), custom_call_target="tpu_custom_call" | custom-call | tf_op jit(solution)/shard_map/mix_points/pallas_call | solution.py:262
  88.4 34.3 %all_to_all.10 = f32[32,72,128]{2,1,0:T(8,128)S(1)} all-to-all(f32[32,72,128]{2,1,0:T(8,128)} %mix_points.1), channel_id=1, replica_groups=mesh['energy'=8,'momentum'=4] {'energy','momentum'}, dimensions={0} | all-to-all | bytes 2359296 | tf_op jit(solution)/shard_map/all_to_all | solution.py:302
  122.7 1.0 copy.17
Async XLA Ops:
  45.4 7.3 %copy-start.1 = (f32[6,2,4,4]{0,3,2,1:T(4,128)S(1)}, f32[6,2,4,4]{0,3,2,1:T(4,128)}, u32[]{:S(2)}) copy-start(f32[6,2,4,4]{0,3,2,1:T(4,128)} %param.13) | copy-start | bytes 2308
  45.4 7.3 %copy-start.2 = (s32[6]{0:T(128)S(1)}, s32[6]{0:T(128)}, u32[]{:S(2)}) copy-start(s32[6]{0:T(128)} %param.12) | copy-start | bytes 76
  45.4 36.4 %all-to-all-start = ((f32[32,72,128]{2,1,0:T(8,128)}), f32[32,72,128]{2,1,0:T(8,128)S(1)}, u32[]{:S(2)}, u32[]{:S(2)}) async-start(f32[32,72,128]{2,1,0:T(8,128)} %bitcast.36), calls=%async_computation | async-start | bytes 2359296 | tf_op jit(solution)/shard_map/all_to_all | solution.py:300
  81.8 1.0 copy-start
